TPU v7x, 32 devices: a whole 2x2x4 slice. The times are simulated.
32 devices in a mesh: mem: 16 (over z, x, core), bal: 2 (over y).
Axes of the slice: x: 2, y: 2, z: 4, core: 2. Of those that a mesh axis runs over, the one named last changes fastest.
Arguments:
- background_trials: bfloat16 [256, 64, 256], P('mem', 'bal'), may hold values from -6 to 6
- mapped_readings: bfloat16 [256, 64, 2048], P('mem', 'bal'), may hold values from -6 to 6
- measured_data: float32 [64, 2048], P('bal'), may hold values from -9 to 9
- inverse_error_variance: float32 [64, 2048], P('bal'), may hold values from 0.05 to 1
- measured_row_tally: int32 [64], P('bal'), may hold values from 16 to 2032, as said below
Outputs:
- analysis: bfloat16 [256, 64, 256], P('mem', 'bal')
Inputs may be any that keep to these rules, and one draw needn't show every extreme that they name: measured_row_tally[p] live rows, the first ones of patch p's block; in each aligned group of 2 consecutive patches the counts sum to at most 2048, and some group sums to exactly 2048.
All inputs are finite; a program needn't handle non-finite values.
Results may differ from a plain program's by a relative error of at most 0.0057.
Values may be sent and summed in bfloat16 or wider, within the bound.
A program may use at most 64 MiB of HBM per device.

v0:
```python
import jax
import jax.numpy as jnp
from jax import lax
from jax.sharding import PartitionSpec as P

NS_ITERS = 7


def prepare(ens, value, prec, count):
    rows = lax.iota(jnp.int32, ens.shape[1])
    mask = (rows < count).astype(jnp.float32)
    weight = mask * jnp.sqrt(prec)
    obs_mean = jnp.mean(ens, axis=0, dtype=jnp.float32)
    scaled = ((ens.astype(jnp.float32) - obs_mean) * weight).astype(jnp.bfloat16)
    misfit = weight * (value - obs_mean)
    vector = jnp.dot(scaled.astype(jnp.float32), misfit, precision=lax.Precision.HIGHEST)
    return (scaled, vector)


def complete_step(gram, vector, region_variables):
    members = gram.shape[0]
    identity = jnp.eye(members, dtype=jnp.float32)
    amat = gram + (members - 1.0) * identity
    frobenius = jnp.sqrt(jnp.sum(amat * amat))
    iterate = amat / frobenius
    inverse = identity
    for step in range(NS_ITERS):
        middle = 1.5 * identity - 0.5 * jnp.dot(inverse, iterate, precision=lax.Precision.HIGHEST)
        iterate = jnp.dot(iterate, middle, precision=lax.Precision.HIGHEST)
        inverse = jnp.dot(middle, inverse, precision=lax.Precision.HIGHEST)
    spread = jnp.sqrt((members - 1.0) / frobenius) * inverse
    inner = jnp.dot(inverse, vector, precision=lax.Precision.HIGHEST)
    mean_weights = jnp.dot(inverse, inner, precision=lax.Precision.HIGHEST) / frobenius
    transform = (spread + mean_weights[:, None]).astype(jnp.bfloat16)
    state_mean = jnp.mean(region_variables, axis=0, dtype=jnp.float32)
    perturb = (region_variables.astype(jnp.float32) - state_mean).astype(jnp.bfloat16)
    moved = jnp.dot(transform.T, perturb, preferred_element_type=jnp.float32)
    return (state_mean + moved).astype(jnp.bfloat16)


def on_device(
    background_trials, mapped_readings, measured_data, inverse_error_variance, measured_row_tally
):
    partner_processors = lax.axis_size("mem")
    region_batch = background_trials.shape[1] // partner_processors
    offset = lax.axis_index("mem") * region_batch
    value = lax.dynamic_slice_in_dim(measured_data, offset, region_batch, 0)
    prec = lax.dynamic_slice_in_dim(inverse_error_variance, offset, region_batch, 0)
    count = lax.dynamic_slice_in_dim(measured_row_tally, offset, region_batch, 0)
    region_variables, ens = (
        lax.all_to_all(background_trials, "mem", split_axis=1, concat_axis=0, tiled=True),
        lax.all_to_all(mapped_readings, "mem", split_axis=1, concat_axis=0, tiled=True),
    )
    scaled, vector = jax.vmap(prepare, in_axes=(1, 0, 0, 0))(ens, value, prec, count)
    gram = jnp.einsum("pkr,plr->pkl", scaled, scaled, preferred_element_type=jnp.float32)
    corrected_trials = jax.vmap(complete_step, in_axes=(0, 0, 1), out_axes=1)(
        gram, vector, region_variables
    )
    return lax.all_to_all(corrected_trials, "mem", split_axis=0, concat_axis=1, tiled=True)


def solution(mesh):
    return jax.shard_map(
        on_device,
        mesh=mesh,
        in_specs=(
            P("mem", "bal", None),
            P("mem", "bal", None),
            P("bal", None),
            P("bal", None),
            P("bal"),
        ),
        out_specs=P("mem", "bal", None),
        check_vma=False,
    )
```

profile of v0, /device:TPU:0, one launch (start us, length us, event | category | flops | bytes accessed | tf_op | source)
XLA Modules:
  0.0 107.5 jit_solution(9631848039329427735)
XLA Ops:
  0.0 1.8 %copy.24 = bf16[16,32,256]{2,0,1:T(8,128)(2,1)} copy(bf16[16,32,256]{2,1,0:T(8,128)(2,1)} %param.5) | data formatting | bytes 524288 | tf_op args[0]
  1.8 7.4 %all-to-all-start = ((bf16[16,32,256]{2,0,1:T(8,128)(2,1)}), bf16[16,32,256]{2,0,1:T(8,128)(2,1)S(1)}, u32[]{:S(2)}, u32[]{:S(2)}) async-start(bf16[16,32,256]{2,0,1:T(8,128)(2,1)} %copy.24), calls=%async_computation | async-start | bytes 524288 | tf_op jit(solution)/shard_map/all_to_all | solution.py:51
  9.2 4.1 %copy.26 = bf16[16,32,2048]{2,0,1:T(8,128)(2,1)} copy(bf16[16,32,2048]{2,1,0:T(8,128)(2,1)} %param.6) | data formatting | bytes 4194304 | tf_op args[1]
  13.3 5.9 %all-to-all-done = bf16[16,32,256]{2,0,1:T(8,128)(2,1)S(1)} async-done(((bf16[16,32,256]{2,0,1:T(8,128)(2,1)}), bf16[16,32,256]{2,0,1:T(8,128)(2,1)S(1)}, u32[]{:S(2)}, u32[]{:S(2)}) %all-to-all-start) | async-done | bytes 262176 | tf_op jit(solution)/shard_map/all_to_all | solution.py:51
  19.2 3.7 %all-to-all-start.1 = ((bf16[16,32,2048]{2,0,1:T(8,128)(2,1)}), bf16[16,32,2048]{2,0,1:T(8,128)(2,1)S(1)}, u32[]{:S(2)}, u32[]{:S(2)}) async-start(bf16[16,32,2048]{2,0,1:T(8,128)(2,1)} %copy.26), calls=%async_computation.1 | async-start | bytes 4194304 | tf_op jit(solution)/shard_map/all_to_all | solution.py:52
  23.0 0.7 fusion.25
  24.0 39.8 %all-to-all-done.1 = bf16[16,32,2048]{2,0,1:T(8,128)(2,1)S(1)} async-done(((bf16[16,32,2048]{2,0,1:T(8,128)(2,1)}), bf16[16,32,2048]{2,0,1:T(8,128)(2,1)S(1)}, u32[]{:S(2)}, u32[]{:S(2)}) %all-to-all-start.1) | async-done | bytes 2097184 | tf_op jit(solution)/shard_map/all_to_all | solution.py:52
  63.9 0.8 convert_reduce_fusion
  65.9 1.0 multiply_bitcast_fusion
  67.9 0.8 multiply_reduce_fusion
  69.3 0.7 fusion.29
  70.3 0.7 fusion.14
  71.0 0.7 fusion.36
  72.3 0.7 fusion.13
  73.0 0.7 fusion.38
  74.3 0.7 fusion.12
  76.3 0.7 fusion.11
  77.6 0.8 fusion.41
  78.5 0.7 fusion.10
  79.1 0.7 fusion.44
  80.5 0.7 fusion.9
  81.8 1.7 %fusion.2 = f32[2,1,256]{2,1,0:T(1,128)S(1)} fusion(bf16[256,2,2048]{2,0,1:T(8,128)(2,1)S(1)} %fusion.1, f32[2,2048,1]{1,0,2:T(2,128)S(1)} %get-tuple-element.5), kind=kOutput, calls=%fused_computation.3 | convolution fusion | flops 12582912 | bytes 2115584 | tf_op jit(solution)/shard_map/vmap()/dot_general | solution.py:16
  85.4 21.0 %all_to_all.36 = bf16[256,2,256]{2,1,0:T(2,128)(2,1)S(1)} all-to-all(bf16[256,2,256]{2,1,0:T(2,128)(2,1)S(1)} %copy.31), channel_id=1, replica_groups=mesh['mem'=16,'bal'=2] {'mem'}, dimensions={0} | all-to-all | bytes 524288 | tf_op jit(solution)/shard_map/all_to_all | solution.py:59
  106.7 0.8 all_to_all.32
  (35 shorter events, 10.2 us)
Async XLA Ops:
  1.8 17.4 %all-to-all-start = ((bf16[16,32,256]{2,0,1:T(8,128)(2,1)}), bf16[16,32,256]{2,0,1:T(8,128)(2,1)S(1)}, u32[]{:S(2)}, u32[]{:S(2)}) async-start(bf16[16,32,256]{2,0,1:T(8,128)(2,1)} %copy.24), calls=%async_computation | async-start | bytes 524288 | tf_op jit(solution)/shard_map/all_to_all | solution.py:51
  13.3 9.7 %copy-start.1 = (s32[32]{0:T(128)S(1)}, s32[32]{0:T(128)}, u32[]{:S(2)}) copy-start(s32[32]{0:T(128)} %param.9) | copy-start | bytes 388
  19.2 44.6 %all-to-all-start.1 = ((bf16[16,32,2048]{2,0,1:T(8,128)(2,1)}), bf16[16,32,2048]{2,0,1:T(8,128)(2,1)S(1)}, u32[]{:S(2)}, u32[]{:S(2)}) async-start(bf16[16,32,2048]{2,0,1:T(8,128)(2,1)} %copy.26), calls=%async_computation.1 | async-start | bytes 4194304 | tf_op jit(solution)/shard_map/all_to_all | solution.py:52
  66.9 1.0 copy-start
where the time goes:
time: 108 us; the launch traced here: 107 us
  waiting for transfers between devices  45.7 us (42%)
  blocking collectives  21 us (19%)
  matrix products  17 us (16%)
  starting transfers between devices  11.1 us (10%)
  local copies, waits for them, and re-layouts  8.38 us (8%)
  other arithmetic  3.99 us (4%)
    all_to_all x1, waiting for transfers between devices, on_device(): lax.all_to_all(mapped_readings, 'mem', split_axis=1, concat_axis=0, tiled...  39.8 us
    all_to_all x1, blocking collectives, on_device(): lax.all_to_all(corrected_trials, 'mem', split_axis=0, concat_axis=1, tile...  21 us
    all_to_all x1, starting transfers between devices, on_device(): lax.all_to_all(background_trials, 'mem', split_axis=1, concat_axis=0, til...  7.39 us
    unnamed x6, local copies, waits for them, and re-layouts  6.28 us
    all_to_all x1, waiting for transfers between devices, on_device(): lax.all_to_all(background_trials, 'mem', split_axis=1, concat_axis=0, til...  5.91 us
    dot_general x7, matrix products, complete_step(): inverse = jnp.dot(middle, inverse, precision=lax.Precision.HIGHEST)  4.5 us
    dot_general x7, matrix products, complete_step(): jnp.dot(inverse, iterate, precision=lax.Precision.HIGHEST)  4.48 us
    dot_general x6, matrix products, complete_step(): iterate = jnp.dot(iterate, middle, precision=lax.Precision.HIGHEST)  3.95 us
  transfers between devices with their start and end apart: 2, of which 2 were waited for; matrix products, arithmetic and copies ran while one was open for 5% of the time, Pallas kernels for 0%

commit v1 on v0

v1 whole, which is shorter than its diff:
```python
import functools

import jax
import jax.numpy as jnp
from jax import lax
from jax.experimental import pallas as pl
from jax.experimental.pallas import tpu as pltpu
from jax.sharding import PartitionSpec as P

NS_ITERS = 7
BLOCK = 256
LANES = 128
CHUNKS = 4
F32, BF16 = jnp.float32, jnp.bfloat16
NN = (((1,), (0,)), ((), ()))
NT = (((1,), (1,)), ((), ()))


def mm(a, b, dims=NN):
    return lax.dot_general(a, b, dims, preferred_element_type=F32)


def split(a):
    high = a.astype(BF16)
    return high, (a - high.astype(F32)).astype(BF16)


def mm3(a, b):
    return mm(a[0], b[0]) + mm(a[0], b[1]) + mm(a[1], b[0])


def kernel(
    n, own, patches, cnt, x_hbm, bg_hbm, md_hbm, iev_hbm, out,
    x_v, bg_v, md_v, iev_v, a_f, b_f, bg_f, sbuf, rbuf, bgs, bgr, outs, gram, vec, high, low, ens_f,
    load_sem, send_sem, recv_sem, bg_send, bg_recv, out_send, out_recv,
):
    rows = x_v.shape[1]
    dim = bg_v.shape[1]
    members = n * own
    span = rows // CHUNKS
    blocks = rows // BLOCK
    me = lax.axis_index("mem")

    order = []
    for c in range(CHUNKS // 2):
        order += [c, CHUNKS - 1 - c]

    def lanes(c):
        return pl.ds(c * span, span)

    loads = {}
    for c in order:
        loads[c] = pltpu.make_async_copy(x_hbm.at[:, lanes(c)], x_v.at[:, lanes(c)], load_sem.at[c])
        loads[c].start()
    others = []
    for k, (src, dst) in enumerate(((iev_hbm, iev_v), (md_hbm, md_v), (bg_hbm, bg_v))):
        others.append(pltpu.make_async_copy(src, dst, load_sem.at[CHUNKS + k]))
        others[-1].start()

    barrier = pltpu.get_barrier_semaphore()

    def greet(d, _):
        pl.semaphore_signal(barrier, inc=1, device_id={"mem": lax.rem(me + d, n)})
        return 0

    lax.fori_loop(1, n, greet, 0)

    flip = (
        lax.broadcasted_iota(jnp.int32, (BLOCK, BLOCK), 0)
        + lax.broadcasted_iota(jnp.int32, (BLOCK, BLOCK), 1)
        == BLOCK - 1
    ).astype(F32)
    flip16 = flip.astype(BF16)
    slot = lax.broadcasted_iota(jnp.int32, (1, span), 1)

    def pack(c, q):
        for k in range(span // LANES):
            at = c * span + k * LANES
            first = a_f[at // LANES, pl.ds(2 * q, own, stride=patches), :]
            second = b_f[at // LANES, pl.ds(2 * q + 1, own, stride=patches), :]
            live = slot[:, :LANES] + at < cnt[2 * q]
            sbuf[c, q, :, pl.ds(k * LANES, LANES)] = jnp.where(live, first, second).astype(BF16)

    def remote(src, dst, ssem, rsem, q):
        return pltpu.make_async_remote_copy(
            src_ref=src, dst_ref=dst, send_sem=ssem, recv_sem=rsem, device_id={"mem": q}
        )

    loaded = set()
    for step, c in enumerate(order):
        for need in (c, CHUNKS - 1 - c):
            if need not in loaded:
                loads[need].wait()
                loaded.add(need)
        for k in range(c * span // LANES, (c + 1) * span // LANES):
            a_f[k] = x_v[:, pl.ds(k * LANES, LANES)].astype(F32)
        for k in range(c * span // BLOCK, (c + 1) * span // BLOCK):
            source = x_v[:, pl.ds((blocks - 1 - k) * BLOCK, BLOCK)]
            turned = mm(source, flip16)
            for i in range(BLOCK // LANES):
                b_f[k * BLOCK // LANES + i] = turned[:, i * LANES : (i + 1) * LANES]
        if step == 0:
            pl.semaphore_wait(barrier, n - 1)

        def send(d, _, c=c):
            q = lax.rem(me + d, n)
            pack(c, q)
            remote(sbuf.at[c, q], rbuf.at[c, me], send_sem.at[c], recv_sem.at[c], q).start()
            return 0

        lax.fori_loop(1, n, send, 0)
        pack(c, me)
        pltpu.make_async_copy(sbuf.at[c, me], rbuf.at[c, me], recv_sem.at[c]).start()

    for copy in others:
        copy.wait()
    for i in range(dim // LANES):
        bg_f[i] = bg_v[:, pl.ds(i * LANES, LANES)].astype(F32)

    def pack_state(q):
        for k in range(2):
            for i in range(dim // LANES):
                block = bg_f[i, pl.ds(2 * q + k, own, stride=patches), :].astype(BF16)
                bgs[q, :, pl.ds(k * dim + i * LANES, LANES)] = block

    def send_state(d, _):
        q = lax.rem(me + d, n)
        pack_state(q)
        remote(bgs.at[q], bgr.at[me], bg_send, bg_recv, q).start()
        return 0

    lax.fori_loop(1, n, send_state, 0)
    pack_state(me)
    pltpu.make_async_copy(bgs.at[me], bgr.at[me], bg_recv).start()

    count_a, count_b = cnt[2 * me], cnt[2 * me + 1]

    def gather_members(block):
        if own % 16 == 0:
            return block.reshape(members, block.shape[2]).astype(F32)
        for k in range(n):
            ens_f[pl.ds(k * own, own), pl.ds(0, block.shape[2])] = block[k].astype(F32)
        return ens_f[:, pl.ds(0, block.shape[2])]

    top = lax.broadcasted_iota(jnp.int32, (8, span), 0)
    for step, c in enumerate(order):
        pos = slot + c * span
        in_a = pos < count_a
        in_b = jnp.logical_and(pos >= count_a, rows - 1 - pos < count_b)
        pair = jnp.where(
            top == 0,
            iev_v[pl.ds(2 * me + 1, 1), lanes(CHUNKS - 1 - c)],
            md_v[pl.ds(2 * me + 1, 1), lanes(CHUNKS - 1 - c)],
        )
        inner_blocks = span // BLOCK
        turned = jnp.concatenate(
            [
                lax.dot_general(
                    pair[:, (inner_blocks - 1 - k) * BLOCK : (inner_blocks - k) * BLOCK], flip, NN,
                    precision=lax.Precision.HIGHEST, preferred_element_type=F32,
                )
                for k in range(inner_blocks)
            ],
            axis=1,
        )
        prec = jnp.where(in_a, iev_v[pl.ds(2 * me, 1), lanes(c)], turned[0:1])
        value = jnp.where(in_a, md_v[pl.ds(2 * me, 1), lanes(c)], turned[1:2])
        root = jnp.sqrt(prec)
        pltpu.make_async_copy(rbuf.at[c], rbuf.at[c], recv_sem.at[c]).wait()
        ens = gather_members(rbuf[c])
        mean = jnp.sum(ens, axis=0, keepdims=True) * (1.0 / members)
        centred = ens - mean
        gap = value - mean
        for k, live in enumerate((in_a, in_b)):
            weight = jnp.where(live, root, 0.0)
            scaled = (centred * weight).astype(BF16)
            misfit = weight * gap
            h, l = split(misfit)
            r = misfit - h.astype(F32) - l.astype(F32)
            parts = jnp.where(top == 0, h.astype(F32), jnp.where(top == 1, l.astype(F32), jnp.where(top == 2, r, 0.0)))
            g = mm(scaled, scaled, NT)
            v = mm(parts.astype(BF16), scaled, NT)
            if step == 0:
                gram[k], vec[k] = g, v
            else:
                gram[k] += g
                vec[k] += v

    eye = (
        lax.broadcasted_iota(jnp.int32, (members, members), 0)
        == lax.broadcasted_iota(jnp.int32, (members, members), 1)
    ).astype(F32)
    upper, lower = pl.ds(0, members), pl.ds(members, members)
    fros = []
    for k in range(2):
        amat = gram[k] + (members - 1.0) * eye
        fro = jnp.sqrt(jnp.sum(jnp.sum(amat * amat, axis=1, keepdims=True), axis=0, keepdims=True))
        fros.append(fro)
        y = amat / fro
        m = 1.5 * eye - 0.5 * y
        ms = split(m)
        ys = split(mm3(split(y), ms))
        for ref, yk, mk in zip((high, low), ys, ms):
            ref[k, upper] = yk
            ref[k, lower] = mk

    def middle(k):
        y = high[k, upper], low[k, upper]
        z = high[k, lower], low[k, lower]
        return split(1.5 * eye - 0.5 * mm3(z, y))

    def iterate(_, carry):
        ms = [middle(k) for k in range(2)]
        for k in range(2):
            yz = split(mm3((high[k], low[k]), ms[k]))
            high[k], low[k] = yz
        return carry

    lax.fori_loop(1, NS_ITERS - 1, iterate, 0)

    pltpu.make_async_copy(bgr, bgr, bg_recv).wait()
    state = gather_members(bgr[...])
    ms = [middle(k) for k in range(2)]
    for k in range(2):
        z = mm3((high[k, lower], low[k, lower]), ms[k])
        zs = split(z)
        row = jnp.sum(vec[k], axis=0, keepdims=True)
        row = jnp.broadcast_to(row, (8, members))
        weights = mm3(split(mm3(split(row), zs)), zs) / fros[k]
        transform = (jnp.sqrt((members - 1.0) / fros[k]) * z + weights[0:1]).astype(BF16)
        block = state[:, k * dim : (k + 1) * dim]
        state_mean = jnp.sum(block, axis=0, keepdims=True) * (1.0 / members)
        moved = mm(transform, (block - state_mean).astype(BF16))
        result = state_mean + moved
        for q in range(n):
            outs[k, q] = result[q * own : (q + 1) * own].astype(BF16)

        def give(d, _, k=k):
            q = lax.rem(me + d, n)
            remote(outs.at[k, q], out.at[k, me], out_send.at[k], out_recv.at[k], q).start()
            return 0

        lax.fori_loop(1, n, give, 0)
        pltpu.make_async_copy(outs.at[k, me], out.at[k, me], out_recv.at[k]).start()

    rest = pl.ds(0, n - 1)
    for c in order:
        pltpu.make_async_copy(sbuf.at[c, rest], sbuf.at[c, rest], send_sem.at[c]).wait()
    pltpu.make_async_copy(bgs.at[rest], bgs.at[rest], bg_send).wait()
    for k in range(2):
        pltpu.make_async_copy(outs.at[k, rest], outs.at[k, rest], out_send.at[k]).wait()
        pltpu.make_async_copy(out.at[k], out.at[k], out_recv.at[k]).wait()


def on_device(background, readings, measured, precision, tally):
    n = lax.axis_size("mem")
    own, patches, rows = readings.shape
    dim = background.shape[2]
    members = n * own
    span = rows // CHUNKS
    hbm = pl.BlockSpec(memory_space=pltpu.MemorySpace.HBM)
    result = pl.pallas_call(
        functools.partial(kernel, n, own, patches),
        out_shape=jax.ShapeDtypeStruct((2, n, own, dim), BF16),
        in_specs=[pl.BlockSpec(memory_space=pltpu.SMEM)] + [hbm] * 4,
        out_specs=hbm,
        scratch_shapes=[
            pltpu.VMEM((own * patches, rows), BF16),
            pltpu.VMEM((own * patches, dim), BF16),
            pltpu.VMEM((patches, rows), F32),
            pltpu.VMEM((patches, rows), F32),
            pltpu.VMEM((rows // LANES, own * patches, LANES), F32),
            pltpu.VMEM((rows // LANES, own * patches, LANES), F32),
            pltpu.VMEM((dim // LANES, own * patches, LANES), F32),
            pltpu.VMEM((CHUNKS, n, own, span), BF16),
            pltpu.VMEM((CHUNKS, n, own, span), BF16),
            pltpu.VMEM((n, own, 2 * dim), BF16),
            pltpu.VMEM((n, own, 2 * dim), BF16),
            pltpu.VMEM((2, n, own, dim), BF16),
            pltpu.VMEM((2, members, members), F32),
            pltpu.VMEM((2, 8, members), F32),
            pltpu.VMEM((2, 2 * members, members), BF16),
            pltpu.VMEM((2, 2 * members, members), BF16),
            pltpu.VMEM((members, max(span, 2 * dim)) if own % 16 else (8, 128), F32),
            pltpu.SemaphoreType.DMA((CHUNKS + 3,)),
            pltpu.SemaphoreType.DMA((CHUNKS,)),
            pltpu.SemaphoreType.DMA((CHUNKS,)),
            pltpu.SemaphoreType.DMA,
            pltpu.SemaphoreType.DMA,
            pltpu.SemaphoreType.DMA((2,)),
            pltpu.SemaphoreType.DMA((2,)),
        ],
        compiler_params=pltpu.CompilerParams(
            collective_id=0, has_side_effects=True, vmem_limit_bytes=56 * 1024 * 1024
        ),
    )(
        tally,
        readings.reshape(own * patches, rows),
        background.reshape(own * patches, dim),
        measured,
        precision,
    )
    return result.transpose(2, 1, 0, 3).reshape(own, patches, dim)


def solution(mesh):
    return jax.shard_map(
        on_device,
        mesh=mesh,
        in_specs=(
            P("mem", "bal", None),
            P("mem", "bal", None),
            P("bal", None),
            P("bal", None),
            P("bal"),
        ),
        out_specs=P("mem", "bal", None),
        check_vma=False,
    )
```

time: 108 us -> 50.4 us (0.47)
  Pallas kernels: 0 us -> 48.4 us
  waiting for transfers between devices: 45.7 us -> 0 us
  blocking collectives: 21 us -> 0 us
  matrix products: 17 us -> 0 us
  starting transfers between devices: 11.1 us -> 0 us
  local copies, waits for them, and re-layouts: 8.38 us -> 1.75 us
  other arithmetic: 3.99 us -> 0 us
    pallas_call x0 -> x1, Pallas kernels: none -> 48.4 us  [on_device(): pl.pallas_call(functools.partial(kernel, n, own, patches), out_shape=jax....]
    all_to_all x2 -> x0, waiting for transfers between devices: 45.7 us -> none  [the longest x1 39.8 us: on_device(): lax.all_to_all(mapped_readings, 'mem', split_axis=1, concat_axis=0, tiled...]
    all_to_all x1 -> x0, blocking collectives: 21 us -> none  [on_device(): lax.all_to_all(corrected_trials, 'mem', split_axis=0, concat_axis=1, tile...]
    dot_general x25 -> x0, matrix products: 17 us -> none  [the longest x7 4.5 us: complete_step(): inverse = jnp.dot(middle, inverse, precision=lax.Precision.HIGHEST)]
    all_to_all x2 -> x0, starting transfers between devices: 11.1 us -> none  [the longest x1 7.39 us: on_device(): lax.all_to_all(background_trials, 'mem', split_axis=1, concat_axis=0, til...]
    unnamed x6 -> x0, local copies, waits for them, and re-layouts: 6.28 us -> none
    mul x3 -> x0, other arithmetic: 1.69 us -> none  [the longest x1 0.96 us: prepare(): misfit = weight * (value - obs_mean)]
    convert_element_type x4 -> x0, other arithmetic: 1.18 us -> none  [the longest x1 0.56 us: prepare(): ((ens.astype(jnp.float32) - obs_mean) * weight).astype(jnp.bfloat16)]
  transfers between devices with their start and end apart: 2 -> 0, of which waited for: 2 -> 0; matrix products, arithmetic and copies ran while one was open for 5% -> 0% of each run, Pallas kernels for 0% -> 0%
where the time goes in v1:
time: 50.4 us; the launch traced here: 50.2 us
  Pallas kernels  48.4 us (96%)
  local copies, waits for them, and re-layouts  1.75 us (3%)
    pallas_call x1, Pallas kernels, on_device(): pl.pallas_call(functools.partial(kernel, n, own, patches), out_shape=jax....  48.4 us

profile of v1, /device:TPU:0, one launch (start us, length us, event | category | flops | bytes accessed | tf_op | source)
XLA Modules:
  0.0 50.2 jit_solution(14606703615519361464)
XLA Ops:
  0.0 48.4 %shard_map.55 = bf16[2,16,16,256]{3,2,1,0:T(8,128)(2,1)} custom-call(s32[32]{0:T(128)} %cnt.1, bf16[512,2048]{1,0:T(8,128)(2,1)} %bitcast.4, bf16[512,256]{1,0:T(8,128)(2,1)} %bitcast.7, f32[32,2048]{1,0:T(8,128)} %md_hbm.1, f32[32,2048]{1,0:T(8,128)} %iev_hbm.1), custom_call_target="tpu_custom_call" | custom-call | tf_op jit(solution)/shard_map/pallas_call | solution.py:262
  48.5 1.0 %copy.6 = bf16[16,16,2,256]{3,0,2,1:T(8,128)(2,1)S(1)} copy(bf16[16,16,2,256]{3,0,1,2:T(8,128)(2,1)} %bitcast.6) | data formatting | bytes 524288 | tf_op jit(solution)/shard_map/transpose | solution.py:303
  49.4 0.8 %copy.7 = bf16[16,32,256]{2,1,0:T(8,128)(2,1)} copy(bf16[16,32,256]{2,0,1:T(8,128)(2,1)S(1)} %bitcast.5) | data formatting | bytes 524288 | tf_op jit(solution)/shard_map/reshape | solution.py:303

commit v2 on v1

--- a/solution.py
+++ b/solution.py
@@ -11,6 +11,7 @@
 BLOCK = 256
 LANES = 128
 CHUNKS = 4
+COARSE = 3
 F32, BF16 = jnp.float32, jnp.bfloat16
 NN = (((1,), (0,)), ((), ()))
 NT = (((1,), (1,)), ((), ()))
@@ -31,7 +32,7 @@
 
 def kernel(
     n, own, patches, cnt, x_hbm, bg_hbm, md_hbm, iev_hbm, out,
-    x_v, bg_v, md_v, iev_v, a_f, b_f, bg_f, sbuf, rbuf, bgs, bgr, outs, gram, vec, high, low, ens_f,
+    x_v, bg_v, md_v, iev_v, a_f, b_f, bg_f, sbuf, rbuf, bgs, bgr, outs, gram, vec, ens_f,
     load_sem, send_sem, recv_sem, bg_send, bg_recv, out_send, out_recv,
 ):
     rows = x_v.shape[1]
@@ -117,21 +118,22 @@
     for i in range(dim // LANES):
         bg_f[i] = bg_v[:, pl.ds(i * LANES, LANES)].astype(F32)
 
-    def pack_state(q):
-        for k in range(2):
-            for i in range(dim // LANES):
-                block = bg_f[i, pl.ds(2 * q + k, own, stride=patches), :].astype(BF16)
-                bgs[q, :, pl.ds(k * dim + i * LANES, LANES)] = block
-
-    def send_state(d, _):
-        q = lax.rem(me + d, n)
-        pack_state(q)
-        remote(bgs.at[q], bgr.at[me], bg_send, bg_recv, q).start()
-        return 0
-
-    lax.fori_loop(1, n, send_state, 0)
-    pack_state(me)
-    pltpu.make_async_copy(bgs.at[me], bgr.at[me], bg_recv).start()
+    def pack_state(k, q):
+        for i in range(dim // LANES):
+            block = bg_f[i, pl.ds(2 * q + k, own, stride=patches), :].astype(BF16)
+            bgs[k, q, :, pl.ds(i * LANES, LANES)] = block
+
+    for k in range(2):
+
+        def send_state(d, _, k=k):
+            q = lax.rem(me + d, n)
+            pack_state(k, q)
+            remote(bgs.at[k, q], bgr.at[k, me], bg_send.at[k], bg_recv.at[k], q).start()
+            return 0
+
+        lax.fori_loop(1, n, send_state, 0)
+        pack_state(k, me)
+        pltpu.make_async_copy(bgs.at[k, me], bgr.at[k, me], bg_recv.at[k]).start()
 
     count_a, count_b = cnt[2 * me], cnt[2 * me + 1]
 
@@ -171,7 +173,7 @@
         mean = jnp.sum(ens, axis=0, keepdims=True) * (1.0 / members)
         centred = ens - mean
         gap = value - mean
-        for k, live in enumerate((in_a, in_b)):
+        def absorb(k, live, step=step, root=root, gap=gap, centred=centred):
             weight = jnp.where(live, root, 0.0)
             scaled = (centred * weight).astype(BF16)
             misfit = weight * gap
@@ -186,70 +188,59 @@
                 gram[k] += g
                 vec[k] += v
 
+        if step < CHUNKS - 1:
+            absorb(0, in_a)
+            absorb(1, in_b)
+
     eye = (
         lax.broadcasted_iota(jnp.int32, (members, members), 0)
         == lax.broadcasted_iota(jnp.int32, (members, members), 1)
     ).astype(F32)
-    upper, lower = pl.ds(0, members), pl.ds(members, members)
-    fros = []
-    for k in range(2):
+    for k, live in enumerate((in_a, in_b)):
+        absorb(k, live)
         amat = gram[k] + (members - 1.0) * eye
         fro = jnp.sqrt(jnp.sum(jnp.sum(amat * amat, axis=1, keepdims=True), axis=0, keepdims=True))
-        fros.append(fro)
         y = amat / fro
-        m = 1.5 * eye - 0.5 * y
-        ms = split(m)
-        ys = split(mm3(split(y), ms))
-        for ref, yk, mk in zip((high, low), ys, ms):
-            ref[k, upper] = yk
-            ref[k, lower] = mk
-
-    def middle(k):
-        y = high[k, upper], low[k, upper]
-        z = high[k, lower], low[k, lower]
-        return split(1.5 * eye - 0.5 * mm3(z, y))
-
-    def iterate(_, carry):
-        ms = [middle(k) for k in range(2)]
-        for k in range(2):
-            yz = split(mm3((high[k], low[k]), ms[k]))
-            high[k], low[k] = yz
-        return carry
-
-    lax.fori_loop(1, NS_ITERS - 1, iterate, 0)
-
-    pltpu.make_async_copy(bgr, bgr, bg_recv).wait()
-    state = gather_members(bgr[...])
-    ms = [middle(k) for k in range(2)]
-    for k in range(2):
-        z = mm3((high[k, lower], low[k, lower]), ms[k])
+        z = eye
+        for step in range(NS_ITERS - 1):
+            if step < COARSE:
+                yh, zh = y.astype(BF16), z.astype(BF16)
+                e = -0.5 * (mm(zh, yh) if step else y)
+                eh = e.astype(BF16)
+                y = 1.5 * y + mm(yh, eh)
+                z = 1.5 * z + (mm(zh, eh) if step else e)
+            else:
+                ys, zs = split(y), split(z)
+                ms = split(1.5 * eye - 0.5 * mm3(zs, ys))
+                y, z = mm3(ys, ms), mm3(zs, ms)
+        ys, zs = split(y), split(z)
+        z = mm3(zs, split(1.5 * eye - 0.5 * mm3(zs, ys)))
         zs = split(z)
-        row = jnp.sum(vec[k], axis=0, keepdims=True)
-        row = jnp.broadcast_to(row, (8, members))
-        weights = mm3(split(mm3(split(row), zs)), zs) / fros[k]
-        transform = (jnp.sqrt((members - 1.0) / fros[k]) * z + weights[0:1]).astype(BF16)
-        block = state[:, k * dim : (k + 1) * dim]
+        row = jnp.broadcast_to(jnp.sum(vec[k], axis=0, keepdims=True), (8, members))
+        weights = mm3(split(mm3(split(row), zs)), zs) / fro
+        transform = (jnp.sqrt((members - 1.0) / fro) * z + weights[0:1]).astype(BF16)
+        pltpu.make_async_copy(bgr.at[k], bgr.at[k], bg_recv.at[k]).wait()
+        block = gather_members(bgr[k])
         state_mean = jnp.sum(block, axis=0, keepdims=True) * (1.0 / members)
-        moved = mm(transform, (block - state_mean).astype(BF16))
-        result = state_mean + moved
+        result = state_mean + mm(transform, (block - state_mean).astype(BF16))
         for q in range(n):
             outs[k, q] = result[q * own : (q + 1) * own].astype(BF16)
 
         def give(d, _, k=k):
             q = lax.rem(me + d, n)
-            remote(outs.at[k, q], out.at[k, me], out_send.at[k], out_recv.at[k], q).start()
+            remote(outs.at[k, q], out.at[me, k], out_send.at[k], out_recv, q).start()
             return 0
 
         lax.fori_loop(1, n, give, 0)
-        pltpu.make_async_copy(outs.at[k, me], out.at[k, me], out_recv.at[k]).start()
+        pltpu.make_async_copy(outs.at[k, me], out.at[me, k], out_recv).start()
 
     rest = pl.ds(0, n - 1)
     for c in order:
         pltpu.make_async_copy(sbuf.at[c, rest], sbuf.at[c, rest], send_sem.at[c]).wait()
-    pltpu.make_async_copy(bgs.at[rest], bgs.at[rest], bg_send).wait()
     for k in range(2):
+        pltpu.make_async_copy(bgs.at[k, rest], bgs.at[k, rest], bg_send.at[k]).wait()
         pltpu.make_async_copy(outs.at[k, rest], outs.at[k, rest], out_send.at[k]).wait()
-        pltpu.make_async_copy(out.at[k], out.at[k], out_recv.at[k]).wait()
+    pltpu.make_async_copy(out, out, out_recv).wait()
 
 
 def on_device(background, readings, measured, precision, tally):
@@ -261,7 +252,7 @@
     hbm = pl.BlockSpec(memory_space=pltpu.MemorySpace.HBM)
     result = pl.pallas_call(
         functools.partial(kernel, n, own, patches),
-        out_shape=jax.ShapeDtypeStruct((2, n, own, dim), BF16),
+        out_shape=jax.ShapeDtypeStruct((n, 2, own, dim), BF16),
         in_specs=[pl.BlockSpec(memory_space=pltpu.SMEM)] + [hbm] * 4,
         out_specs=hbm,
         scratch_shapes=[
@@ -274,21 +265,19 @@
             pltpu.VMEM((dim // LANES, own * patches, LANES), F32),
             pltpu.VMEM((CHUNKS, n, own, span), BF16),
             pltpu.VMEM((CHUNKS, n, own, span), BF16),
-            pltpu.VMEM((n, own, 2 * dim), BF16),
-            pltpu.VMEM((n, own, 2 * dim), BF16),
+            pltpu.VMEM((2, n, own, dim), BF16),
+            pltpu.VMEM((2, n, own, dim), BF16),
             pltpu.VMEM((2, n, own, dim), BF16),
             pltpu.VMEM((2, members, members), F32),
             pltpu.VMEM((2, 8, members), F32),
-            pltpu.VMEM((2, 2 * members, members), BF16),
-            pltpu.VMEM((2, 2 * members, members), BF16),
-            pltpu.VMEM((members, max(span, 2 * dim)) if own % 16 else (8, 128), F32),
+            pltpu.VMEM((members, max(span, dim)) if own % 16 else (8, 128), F32),
             pltpu.SemaphoreType.DMA((CHUNKS + 3,)),
             pltpu.SemaphoreType.DMA((CHUNKS,)),
             pltpu.SemaphoreType.DMA((CHUNKS,)),
-            pltpu.SemaphoreType.DMA,
-            pltpu.SemaphoreType.DMA,
             pltpu.SemaphoreType.DMA((2,)),
             pltpu.SemaphoreType.DMA((2,)),
+            pltpu.SemaphoreType.DMA((2,)),
+            pltpu.SemaphoreType.DMA,
         ],
         compiler_params=pltpu.CompilerParams(
             collective_id=0, has_side_effects=True, vmem_limit_bytes=56 * 1024 * 1024
@@ -300,7 +289,7 @@
         measured,
         precision,
     )
-    return result.transpose(2, 1, 0, 3).reshape(own, patches, dim)
+    return result.reshape(patches, own, dim).transpose(1, 0, 2)
 
 
 def solution(mesh):

time: 50.4 us -> 50.9 us (level)
  Pallas kernels: 48.4 us -> 49 us
    transpose x1 -> x0, local copies, waits for them, and re-layouts: 0.97 us -> none  [on_device(): return result.transpose(2, 1, 0, 3).reshape(own, patches, dim)]
    reshape x1, local copies, waits for them, and re-layouts: 0.78 us -> 1.73 us  [on_device(): return result.reshape(patches, own, dim).transpose(1, 0, 2)]
    pallas_call x1, Pallas kernels: 48.4 us -> 49 us  [on_device(): pl.pallas_call(functools.partial(kernel, n, own, patches), out_shape=jax....]
where the time goes in v2:
time: 50.9 us; the launch traced here: 50.7 us
  Pallas kernels  49 us (96%)
  local copies, waits for them, and re-layouts  1.73 us (3%)
    pallas_call x1, Pallas kernels, on_device(): pl.pallas_call(functools.partial(kernel, n, own, patches), out_shape=jax....  49 us
    reshape x1, local copies, waits for them, and re-layouts, on_device(): return result.reshape(patches, own, dim).transpose(1, 0, 2)  1.73 us

profile of v2, /device:TPU:0, one launch (start us, length us, event | category | flops | bytes accessed | tf_op | source)
XLA Modules:
  0.0 50.7 jit_solution(2043127030841605489)
XLA Ops:
  0.0 49.0 %shard_map.55 = bf16[16,2,16,256]{3,2,1,0:T(8,128)(2,1)} custom-call(s32[32]{0:T(128)} %cnt.1, bf16[512,2048]{1,0:T(8,128)(2,1)} %bitcast.6, bf16[512,256]{1,0:T(8,128)(2,1)} %bitcast.8, f32[32,2048]{1,0:T(8,128)} %md_hbm.1, f32[32,2048]{1,0:T(8,128)} %iev_hbm.1), custom_call_target="tpu_custom_call" | custom-call | tf_op jit(solution)/shard_map/pallas_call | solution.py:253
  49.0 1.7 %copy.8 = bf16[32,16,256]{2,0,1:T(8,128)(2,1)} copy(bf16[32,16,256]{2,1,0:T(8,128)(2,1)} %bitcast.7) | data formatting | bytes 524288 | tf_op jit(solution)/shard_map/reshape | solution.py:292

commit v3 on v2

--- a/solution.py
+++ b/solution.py
@@ -144,7 +144,7 @@
             ens_f[pl.ds(k * own, own), pl.ds(0, block.shape[2])] = block[k].astype(F32)
         return ens_f[:, pl.ds(0, block.shape[2])]
 
-    top = lax.broadcasted_iota(jnp.int32, (8, span), 0)
+    top = lax.broadcasted_iota(jnp.int32, (16, span), 0)
     for step, c in enumerate(order):
         pos = slot + c * span
         in_a = pos < count_a
@@ -180,45 +180,58 @@
             h, l = split(misfit)
             r = misfit - h.astype(F32) - l.astype(F32)
             parts = jnp.where(top == 0, h.astype(F32), jnp.where(top == 1, l.astype(F32), jnp.where(top == 2, r, 0.0)))
-            g = mm(scaled, scaled, NT)
-            v = mm(parts.astype(BF16), scaled, NT)
+            both = mm(jnp.concatenate([scaled, parts.astype(BF16)], axis=0), scaled, NT)
+            g, v = both[:members], both[members:]
             if step == 0:
                 gram[k], vec[k] = g, v
             else:
                 gram[k] += g
                 vec[k] += v
 
-        if step < CHUNKS - 1:
-            absorb(0, in_a)
-            absorb(1, in_b)
+        absorb(0, in_a)
+        absorb(1, in_b)
 
     eye = (
         lax.broadcasted_iota(jnp.int32, (members, members), 0)
         == lax.broadcasted_iota(jnp.int32, (members, members), 1)
     ).astype(F32)
-    for k, live in enumerate((in_a, in_b)):
-        absorb(k, live)
+    fros, ys, zs = [], [], []
+    for k in range(2):
         amat = gram[k] + (members - 1.0) * eye
         fro = jnp.sqrt(jnp.sum(jnp.sum(amat * amat, axis=1, keepdims=True), axis=0, keepdims=True))
-        y = amat / fro
-        z = eye
-        for step in range(NS_ITERS - 1):
-            if step < COARSE:
-                yh, zh = y.astype(BF16), z.astype(BF16)
-                e = -0.5 * (mm(zh, yh) if step else y)
-                eh = e.astype(BF16)
-                y = 1.5 * y + mm(yh, eh)
-                z = 1.5 * z + (mm(zh, eh) if step else e)
-            else:
-                ys, zs = split(y), split(z)
-                ms = split(1.5 * eye - 0.5 * mm3(zs, ys))
-                y, z = mm3(ys, ms), mm3(zs, ms)
-        ys, zs = split(y), split(z)
-        z = mm3(zs, split(1.5 * eye - 0.5 * mm3(zs, ys)))
-        zs = split(z)
-        row = jnp.broadcast_to(jnp.sum(vec[k], axis=0, keepdims=True), (8, members))
-        weights = mm3(split(mm3(split(row), zs)), zs) / fro
-        transform = (jnp.sqrt((members - 1.0) / fro) * z + weights[0:1]).astype(BF16)
+        fros.append(fro)
+        ys.append(amat / fro)
+        zs.append(eye)
+    for step in range(NS_ITERS - 1):
+        if step < COARSE:
+            yh, zh = [y.astype(BF16) for y in ys], [z.astype(BF16) for z in zs]
+            es = [-0.5 * (mm(zh[k], yh[k]) if step else ys[k]) for k in range(2)]
+            eh = [e.astype(BF16) for e in es]
+            for k in range(2):
+                ys[k] = 1.5 * ys[k] + mm(yh[k], eh[k])
+                zs[k] = 1.5 * zs[k] + (mm(zh[k], eh[k]) if step else es[k])
+        else:
+            y2, z2 = [split(y) for y in ys], [split(z) for z in zs]
+            ms = [split(1.5 * eye - 0.5 * mm3(z2[k], y2[k])) for k in range(2)]
+            for k in range(2):
+                ys[k] = mm3(y2[k], ms[k])
+                zs[k] = mm3(z2[k], ms[k])
+    y2, z2 = [split(y) for y in ys], [split(z) for z in zs]
+    ms = [split(1.5 * eye - 0.5 * mm3(z2[k], y2[k])) for k in range(2)]
+    zs = [mm3(z2[k], ms[k]) for k in range(2)]
+
+    line = lax.broadcasted_iota(jnp.int32, (16, members), 0)
+
+    def times(row, matrix):
+        h, l = split(row)
+        pair = jnp.where(line == 0, h.astype(F32), jnp.where(line == 1, l.astype(F32), 0.0))
+        return jnp.sum(mm(pair.astype(BF16), matrix), axis=0, keepdims=True)
+
+    for k in range(2):
+        fro, z = fros[k], zs[k]
+        zh = z.astype(BF16)
+        weights = times(times(jnp.sum(vec[k], axis=0, keepdims=True), zh), zh) / fro
+        transform = (jnp.sqrt((members - 1.0) / fro) * z + weights).astype(BF16)
         pltpu.make_async_copy(bgr.at[k], bgr.at[k], bg_recv.at[k]).wait()
         block = gather_members(bgr[k])
         state_mean = jnp.sum(block, axis=0, keepdims=True) * (1.0 / members)
@@ -269,7 +282,7 @@
             pltpu.VMEM((2, n, own, dim), BF16),
             pltpu.VMEM((2, n, own, dim), BF16),
             pltpu.VMEM((2, members, members), F32),
-            pltpu.VMEM((2, 8, members), F32),
+            pltpu.VMEM((2, 16, members), F32),
             pltpu.VMEM((members, max(span, dim)) if own % 16 else (8, 128), F32),
             pltpu.SemaphoreType.DMA((CHUNKS + 3,)),
             pltpu.SemaphoreType.DMA((CHUNKS,)),

time: 50.9 us -> 48.3 us (0.949)
  Pallas kernels: 49 us -> 46.4 us
    pallas_call x1, Pallas kernels: 49 us -> 46.4 us  [on_device(): pl.pallas_call(functools.partial(kernel, n, own, patches), out_shape=jax....]
where the time goes in v3:
time: 48.3 us; the launch traced here: 48.2 us
  Pallas kernels  46.4 us (96%)
  local copies, waits for them, and re-layouts  1.73 us (4%)
    pallas_call x1, Pallas kernels, on_device(): pl.pallas_call(functools.partial(kernel, n, own, patches), out_shape=jax....  46.4 us
    reshape x1, local copies, waits for them, and re-layouts, on_device(): return result.reshape(patches, own, dim).transpose(1, 0, 2)  1.73 us

profile of v3, /device:TPU:0, one launch (start us, length us, event | category | flops | bytes accessed | tf_op | source)
XLA Modules:
  0.0 48.2 jit_solution(5172765582896017931)
XLA Ops:
  0.0 46.4 %shard_map.55 = bf16[16,2,16,256]{3,2,1,0:T(8,128)(2,1)} custom-call(s32[32]{0:T(128)} %cnt.1, bf16[512,2048]{1,0:T(8,128)(2,1)} %bitcast.6, bf16[512,256]{1,0:T(8,128)(2,1)} %bitcast.8, f32[32,2048]{1,0:T(8,128)} %md_hbm.1, f32[32,2048]{1,0:T(8,128)} %iev_hbm.1), custom_call_target="tpu_custom_call" | custom-call | tf_op jit(solution)/shard_map/pallas_call | solution.py:266
  46.4 1.7 %copy.8 = bf16[32,16,256]{2,0,1:T(8,128)(2,1)} copy(bf16[32,16,256]{2,1,0:T(8,128)(2,1)} %bitcast.7) | data formatting | bytes 524288 | tf_op jit(solution)/shard_map/reshape | solution.py:305

commit v4 on v3

--- a/solution.py
+++ b/solution.py
@@ -216,6 +216,12 @@
             for k in range(2):
                 ys[k] = mm3(y2[k], ms[k])
                 zs[k] = mm3(z2[k], ms[k])
+    states = []
+    for k in range(2):
+        pltpu.make_async_copy(bgr.at[k], bgr.at[k], bg_recv.at[k]).wait()
+        block = gather_members(bgr[k])
+        state_mean = jnp.sum(block, axis=0, keepdims=True) * (1.0 / members)
+        states.append((state_mean, (block - state_mean).astype(BF16)))
     y2, z2 = [split(y) for y in ys], [split(z) for z in zs]
     ms = [split(1.5 * eye - 0.5 * mm3(z2[k], y2[k])) for k in range(2)]
     zs = [mm3(z2[k], ms[k]) for k in range(2)]
@@ -225,17 +231,15 @@
     def times(row, matrix):
         h, l = split(row)
         pair = jnp.where(line == 0, h.astype(F32), jnp.where(line == 1, l.astype(F32), 0.0))
-        return jnp.sum(mm(pair.astype(BF16), matrix), axis=0, keepdims=True)
-
-    for k in range(2):
-        fro, z = fros[k], zs[k]
-        zh = z.astype(BF16)
-        weights = times(times(jnp.sum(vec[k], axis=0, keepdims=True), zh), zh) / fro
-        transform = (jnp.sqrt((members - 1.0) / fro) * z + weights).astype(BF16)
-        pltpu.make_async_copy(bgr.at[k], bgr.at[k], bg_recv.at[k]).wait()
-        block = gather_members(bgr[k])
-        state_mean = jnp.sum(block, axis=0, keepdims=True) * (1.0 / members)
-        result = state_mean + mm(transform, (block - state_mean).astype(BF16))
+        pair = pair.astype(BF16)
+        return jnp.sum(mm(pair, matrix[0]) + mm(pair, matrix[1]), axis=0, keepdims=True)
+
+    zs2 = [split(z) for z in zs]
+    inner = [times(jnp.sum(vec[k], axis=0, keepdims=True), zs2[k]) for k in range(2)]
+    weights = [times(inner[k], zs2[k]) / fros[k] for k in range(2)]
+    for k in range(2):
+        transform = (jnp.sqrt((members - 1.0) / fros[k]) * zs[k] + weights[k]).astype(BF16)
+        result = states[k][0] + mm(transform, states[k][1])
         for q in range(n):
             outs[k, q] = result[q * own : (q + 1) * own].astype(BF16)
 

time: 48.3 us -> 48.6 us (level)
  no operation moved by 1% of the time
where the time goes in v4:
time: 48.6 us; the launch traced here: 48.4 us
  Pallas kernels  46.7 us (96%)
  local copies, waits for them, and re-layouts  1.73 us (4%)
    pallas_call x1, Pallas kernels, on_device(): pl.pallas_call(functools.partial(kernel, n, own, patches), out_shape=jax....  46.7 us
    reshape x1, local copies, waits for them, and re-layouts, on_device(): return result.reshape(patches, own, dim).transpose(1, 0, 2)  1.73 us

profile of v4, /device:TPU:0, one launch (start us, length us, event | category | flops | bytes accessed | tf_op | source)
XLA Modules:
  0.0 48.4 jit_solution(6164298969232297736)
XLA Ops:
  0.0 46.7 %shard_map.55 = bf16[16,2,16,256]{3,2,1,0:T(8,128)(2,1)} custom-call(s32[32]{0:T(128)} %cnt.1, bf16[512,2048]{1,0:T(8,128)(2,1)} %bitcast.6, bf16[512,256]{1,0:T(8,128)(2,1)} %bitcast.8, f32[32,2048]{1,0:T(8,128)} %md_hbm.1, f32[32,2048]{1,0:T(8,128)} %iev_hbm.1), custom_call_target="tpu_custom_call" | custom-call | tf_op jit(solution)/shard_map/pallas_call | solution.py:270
  46.7 1.7 %copy.8 = bf16[32,16,256]{2,0,1:T(8,128)(2,1)} copy(bf16[32,16,256]{2,1,0:T(8,128)(2,1)} %bitcast.7) | data formatting | bytes 524288 | tf_op jit(solution)/shard_map/reshape | solution.py:309
